TPU v7x, 32 devices: a whole 2x2x4 slice. The times are simulated.
32 devices in a mesh: tok: 4 (over x, core), inc: 2 (over y), outc: 4 (over z).
Axes of the slice: x: 2, y: 2, z: 4, core: 2. Of those that a mesh axis runs over, the one named last changes fastest.
Arguments:
- activations: bfloat16 [2, 1024, 8192], P(None, 'tok', 'inc'), may hold values from -0.119628906 to 0.119628906
- student_out: bfloat16 [2, 1024, 4096], P(None, ('tok', 'inc'), 'outc'), may hold values from -6 to 6
- teacher_out: bfloat16 [2, 1024, 4096], P(None, ('tok', 'inc'), 'outc'), may hold values from -6 to 6
- weight: bfloat16 [2, 4096, 4096], P('inc', 'tok', 'outc'), may hold values from -0.0625 to 0.0625
Outputs:
- input_grad: bfloat16 [2, 1024, 8192], P(None, ('tok', 'outc'), 'inc')
- weight_grad: float32 [2, 4096, 4096], P('inc', 'tok', 'outc')
All inputs are finite; a program needn't handle non-finite values.
Results may differ from a plain program's by a relative error of at most 0.0051.
Values may be sent and summed in bfloat16 or wider, within the bound.
A program may use at most 128 MiB of HBM per device.

v0:
```python
import jax
import jax.numpy as jnp
from jax import lax
from jax.sharding import PartitionSpec as P


def local(activations, student_out, teacher_out, weight):
    difference = (student_out.astype(jnp.float32) - teacher_out.astype(jnp.float32)).astype(
        jnp.bfloat16
    )
    cotangent = lax.all_gather(difference, "inc", axis=1, tiled=True)
    partial_grad = jnp.einsum(
        "mtc,rc->mtr",
        cotangent,
        lax.all_gather(weight, "tok", axis=1, tiled=True)[0],
        preferred_element_type=jnp.float32,
    )
    input_grad = lax.psum_scatter(partial_grad, "outc", scatter_dimension=1, tiled=True).astype(
        jnp.bfloat16
    )
    weight_grad = None
    for batch_idx in range(cotangent.shape[0]):

        def batch_term(start, count, batch_idx=batch_idx):
            columns = activations[batch_idx]
            return jnp.einsum(
                "ti,tc->ic", columns, cotangent[batch_idx], preferred_element_type=jnp.float32
            )

        share = lax.psum_scatter(
            batch_term(jnp.int32(0), lax.axis_size("tok") * weight.shape[1]),
            "tok",
            scatter_dimension=0,
            tiled=True,
        )
        weight_grad = share if weight_grad is None else weight_grad + share
    return (input_grad, weight_grad.reshape(weight.shape))


def solution(mesh):
    placed = (
        P(None, "tok", "inc"),
        P(None, ("tok", "inc"), "outc"),
        P(None, ("tok", "inc"), "outc"),
        P("inc", "tok", "outc"),
    )
    return jax.shard_map(
        local,
        mesh=mesh,
        in_specs=placed,
        out_specs=(P(None, ("tok", "outc"), "inc"), P("inc", "tok", "outc")),
        check_vma=False,
    )
```

profile of v0, /device:TPU:25, one launch (start us, length us, event | category | flops | bytes accessed | tf_op | source)
XLA Modules:
  0.0 388.2 jit_solution(16638279398995200591)
XLA Ops:
  7.2 0.0 all-gather.3.cloned.1.call-start
  7.2 2.2 subtract_convert_fusion
  9.4 0.0 all-gather.3.cloned.1.call-update
  9.4 0.0 all-gather.5.cloned.1.call-start
  9.5 0.7 all-gather.5.cloned.1.call-update
  10.2 0.0 reduce-scatter.3.cloned.1.call-start
  10.2 22.0 %all-gather.3.cloned.1.call-done = bf16[2,256,1024]{2,1,0:T(8,128)(2,1)} async-done(((bf16[2,128,1024]{2,1,0:T(8,128)(2,1)}), bf16[2,256,1024]{2,1,0:T(8,128)(2,1)}) %all-gather.3.cloned.1.call-update) | async-done | bytes 1048592 | tf_op jit(solution)/shard_map/all_gather | solution.py:11
  32.2 60.4 %all-gather.5.cloned.1.call-done = bf16[1,4096,1024]{2,1,0:T(8,128)(2,1)} async-done(((bf16[1,1024,1024]{2,1,0:T(8,128)(2,1)}), bf16[1,4096,1024]{2,1,0:T(8,128)(2,1)}) %all-gather.5.cloned.1.call-update) | async-done | bytes 8388624 | tf_op jit(solution)/shard_map/all_gather | solution.py:15
  92.6 11.5 %fusion = f32[2,256,4096]{2,1,0:T(8,128)} fusion(bf16[2,256,1024]{2,1,0:T(8,128)(2,1)} %all-gather.3.cloned.1.call-done, bf16[1,4096,1024]{2,1,0:T(8,128)(2,1)} %all-gather.5.cloned.1.call-done), kind=kOutput, calls=%fused_computation.1 | convolution fusion | flops 4294967296 | bytes 17825792 | tf_op jit(solution)/shard_map/mtc,rc->mtr/dot_general | solution.py:12
  104.1 0.0 copy-start
  104.1 0.0 reduce-scatter.3.cloned.1.call-update
  104.2 0.0 reduce-scatter.5.cloned.1.call-start
  104.2 1.1 copy-done
  105.4 4.0 %fusion.3 = f32[1024,4096]{1,0:T(8,128)S(1)} fusion(bf16[2,256,4096]{2,1,0:T(8,128)(2,1)} %param.4, bf16[2,256,1024]{2,1,0:T(8,128)(2,1)S(1)} %copy-done), kind=kOutput, calls=%fused_computation.4 | convolution fusion | flops 2147483648 | bytes 19398656 | tf_op jit(solution)/shard_map/ti,tc->ic/dot_general | solution.py:26
  109.4 10.2 %add_bitcast_fusion = f32[4096,1024]{0,1:T(8,128)} fusion(f32[1024,4096]{1,0:T(8,128)S(1)} %fusion.3, bf16[2,256,4096]{2,1,0:T(8,128)(2,1)} %param.4, bf16[2,256,1024]{2,1,0:T(8,128)(2,1)S(1)} %copy-done), kind=kOutput, calls=%fused_computation | convolution fusion | flops 2151677952 | bytes 36175872 | tf_op jit(solution)/shard_map/ti,tc->ic/dot_general | solution.py:26
  119.6 0.0 reduce-scatter.5.cloned.1.call-update
  119.6 128.4 %reduce-scatter.3.cloned.1.call-done = f32[2,64,4096]{2,1,0:T(8,128)} async-done(((f32[2,256,4096]{2,1,0:T(8,128)}), f32[2,64,4096]{2,1,0:T(8,128)}) %reduce-scatter.3.cloned.1.call-update) | async-done | bytes 2097168 | tf_op jit(solution)/shard_map/reduce_scatter | solution.py:18
  248.0 2.7 convert_element_type.15
  250.7 125.6 %reduce-scatter.5.cloned.1.call-done = f32[1024,1024]{0,1:T(8,128)} async-done(((f32[4096,1024]{0,1:T(8,128)}), f32[1024,1024]{0,1:T(8,128)}) %reduce-scatter.5.cloned.1.call-update) | async-done | bytes 4194320 | tf_op jit(solution)/shard_map/reduce_scatter | solution.py:30
  376.3 5.3 %copy.6 = f32[1,1024,1024]{2,1,0:T(8,128)} copy(f32[1,1024,1024]{1,2,0:T(8,128)} %bitcast.20) | data formatting | bytes 8388608
Async XLA Ops:
  7.2 25.1 %all-gather.3.cloned.1.call-start = ((), (), s32[]{:S(2)}) async-start(), calls=%async_computation.2 | async-start | bytes 1572864 | tf_op jit(solution)/shard_map/all_gather | solution.py:11
  9.4 83.2 %all-gather.5.cloned.1.call-start = ((), (), s32[]{:S(2)}) async-start(), calls=%async_computation.3 | async-start | bytes 10485760 | tf_op jit(solution)/shard_map/all_gather | solution.py:15
  10.2 237.9 %reduce-scatter.3.cloned.1.call-start = ((), (), s32[]{:S(2)}) async-start(), calls=%async_computation.4 | async-start | bytes 10485760 | tf_op jit(solution)/shard_map/reduce_scatter | solution.py:18
  104.1 1.2 copy-start
  104.2 272.2 %reduce-scatter.5.cloned.1.call-start = ((), (), s32[]{:S(2)}) async-start(), calls=%async_computation.5 | async-start | bytes 20971520 | tf_op jit(solution)/shard_map/reduce_scatter | solution.py:30
Sparse Core Ops, SparseCore 0:
  10.1 22.0 all-gather.2
  33.8 58.8 all-gather.4
  104.3 143.7 reduce-scatter.2
  250.5 125.8 reduce-scatter.4
where the time goes:
time: 390 us; the launch traced here: 388 us
  waiting for transfers between devices  337 us (86%)
  matrix products  25.7 us (7%)
  between operations  13.8 us (4%)
  local copies, waits for them, and re-layouts  6.49 us (2%)
  other arithmetic  4.88 us (1%)
    reduce_scatter x1, waiting for transfers between devices, local(): lax.psum_scatter(partial_grad, 'outc', scatter_dimension=1, tiled=True)  128 us
    reduce_scatter x1, waiting for transfers between devices, local(): lax.psum_scatter(batch_term(jnp.int32(0), lax.axis_size('tok') * weight.s...  126 us
    all_gather x1, waiting for transfers between devices, local(): lax.all_gather(weight, 'tok', axis=1, tiled=True)[0]  60.4 us
    all_gather x1, waiting for transfers between devices, local(): cotangent = lax.all_gather(difference, 'inc', axis=1, tiled=True)  22 us
    dot_general x2, matrix products, batch_term(): jnp.einsum('ti,tc->ic', columns, cotangent[batch_idx], preferred_element_...  14.2 us
    dot_general x1, matrix products, local(): jnp.einsum('mtc,rc->mtr', cotangent, lax.all_gather(weight, 'tok', axis=1...  11.5 us
  transfers between devices with their start and end apart: 4, of which 4 were waited for; matrix products, arithmetic and copies ran while one was open for 4% of the time, Pallas kernels for 0%

commit v1 on v0

v1 whole, which is shorter than its diff:
```python
import functools

import jax
import jax.numpy as jnp
from jax import lax
from jax.experimental import pallas as pl
from jax.experimental.pallas import tpu as pltpu
from jax.sharding import PartitionSpec as P

MESH = pl.DeviceIdType.MESH


def kernel(
    sizes,
    act,
    student,
    teacher,
    weight,
    dx_out,
    dw_out,
    cot,
    acts,
    part,
    recv,
    sendbuf,
    landing,
    dw,
    w,
    cot_core_s,
    cot_tok_s,
    cot_inc_s,
    cot_r,
    act_s,
    act_r,
    line_s,
    line_r,
    fin_s,
    fin_r,
    out_s,
    misc_s,
):
    n_tok, n_inc, n_out = sizes
    pairs = n_tok // 2
    per_block = n_out // n_inc
    blocks = n_tok * n_inc
    feats = dw.shape[0]
    i, j, k = lax.axis_index("tok"), lax.axis_index("inc"), lax.axis_index("outc")
    p, c = i // 2, i % 2
    f_tile = min(256, feats)

    def tok_at(dp, dc):
        return lax.rem(p + dp, pairs) * 2 + lax.rem(c + dc, 2)

    def inc_at(dj):
        return lax.rem(j + dj, n_inc)

    barrier = pltpu.get_barrier_semaphore()
    for d in range(1, n_tok):
        pl.semaphore_signal(
            barrier, inc=1, device_id={"tok": lax.rem(i + d, n_tok)}, device_id_type=MESH
        )
    for d in range(1, n_inc):
        pl.semaphore_signal(barrier, inc=1, device_id={"inc": inc_at(d)}, device_id_type=MESH)

    @pl.when(k > 0)
    def _():
        pl.semaphore_signal(barrier, inc=1, device_id={"outc": k - 1}, device_id_type=MESH)

    @pl.when(k < n_out - 1)
    def _():
        pl.semaphore_signal(barrier, inc=1, device_id={"outc": k + 1}, device_id_type=MESH)

    own = i * n_inc + j
    w_copy = pltpu.make_async_copy(weight, w, misc_s.at[0])
    w_copy.start()
    act_copy = pltpu.make_async_copy(
        act.at[:, :, pl.ds(pl.multiple_of(i * feats, feats), feats)], acts.at[i], misc_s.at[1]
    )
    act_copy.start()
    cot[own] = (student[...].astype(jnp.float32) - teacher[...].astype(jnp.float32)).astype(
        jnp.bfloat16
    )

    @pl.loop(0, feats // f_tile)
    def _(t):
        rows = pl.ds(pl.multiple_of(t * f_tile, f_tile), f_tile)
        dw[rows, :] = jnp.zeros((f_tile, dw.shape[1]), jnp.float32)

    edges = jnp.where(k > 0, 1, 0) + jnp.where(k < n_out - 1, 1, 0)
    pl.semaphore_wait(barrier, n_tok - 1 + n_inc - 1 + edges)

    def cot_copy(g, sem, device):
        return pltpu.make_async_remote_copy(
            src_ref=cot.at[g],
            dst_ref=cot.at[g],
            send_sem=sem,
            recv_sem=cot_r.at[g],
            device_id=device,
            device_id_type=MESH,
        )

    core = {"tok": tok_at(0, 1)}

    def to_core(g):
        return cot_copy(g, cot_core_s.at[g], core)

    def to_tok(dp):
        return cot_copy(own, cot_tok_s.at[dp], {"tok": tok_at(dp, 0)})

    def to_inc(dp, dj):
        g = tok_at(dp, 0) * n_inc + j
        return cot_copy(g, cot_inc_s.at[dp * n_inc + dj], {"inc": inc_at(dj)})

    def act_send(dp, dc):
        to = tok_at(dp, dc)
        return pltpu.make_async_remote_copy(
            src_ref=act.at[:, :, pl.ds(pl.multiple_of(to * feats, feats), feats)],
            dst_ref=acts.at[i],
            send_sem=act_s.at[dp * 2 + dc],
            recv_sem=act_r.at[i],
            device_id={"tok": to},
            device_id_type=MESH,
        )

    to_core(own).start()
    for dp in range(1, pairs):
        to_tok(dp).start()
    for dj in range(1, n_inc):
        to_inc(0, dj).start()
    for dp in range(pairs):
        for dc in range(2):
            if dp or dc:
                act_send(dp, dc).start()
    w_copy.wait()

    def block_of(b):
        dc, rest = b % 2, b // 2
        dj, dp = rest % n_inc, rest // n_inc
        to, jj = tok_at(dp, dc), inc_at(dj)
        return to, jj, to * n_inc + jj, dc

    def line_copy(item, down):
        return pltpu.make_async_remote_copy(
            src_ref=sendbuf.at[item],
            dst_ref=recv.at[down, item],
            send_sem=line_s.at[item],
            recv_sem=line_r.at[down, item],
            device_id={"outc": k + 1 - 2 * down},
            device_id_type=MESH,
        )

    def line_wait(item, down):
        pltpu.make_async_remote_copy(
            src_ref=sendbuf.at[item],
            dst_ref=recv.at[down, item],
            send_sem=line_s.at[item],
            recv_sem=line_r.at[down, item],
            device_id={"outc": lax.rem(k + 1, n_out)},
            device_id_type=MESH,
        ).wait_recv()

    at_edge = (k == 0) | (k == n_out - 1)

    def compute(b):
        to, jj, g, dc = block_of(b)

        @pl.when(dc == 1)
        def _():
            to_core(g).wait_recv()

        rows = cot[g]
        n_mb, n_rows, depth = rows.shape
        rows = rows.reshape(n_mb * n_rows, depth)

        @pl.loop(0, feats // f_tile)
        def _(t):
            cols = pl.ds(pl.multiple_of(t * f_tile, f_tile), f_tile)
            res = lax.dot_general(
                cot[g].reshape(n_mb * n_rows, depth),
                w[0, cols, :],
                (((1,), (1,)), ((), ())),
                preferred_element_type=jnp.float32,
            ).reshape(n_mb, per_block, n_rows // per_block, f_tile)
            for s in range(per_block):
                part[g * per_block + s, :, :, cols] = res[:, s]

        @pl.when(at_edge)
        def _():
            @pl.loop(0, per_block)
            def _(s):
                item = g * per_block + s
                target = jj * per_block + s

                @pl.when(target != k)
                def _():
                    sendbuf[item] = part[item].astype(jnp.bfloat16)
                    line_copy(item, jnp.where(target < k, 1, 0)).start()

    def fin_copy(to):
        return pltpu.make_async_remote_copy(
            src_ref=sendbuf.at[to * n_out + k],
            dst_ref=landing.at[i],
            send_sem=fin_s.at[to],
            recv_sem=fin_r.at[i],
            device_id={"tok": to},
            device_id_type=MESH,
        )

    def relay(b):
        to, jj, g, dc = block_of(b)

        @pl.loop(0, per_block)
        def _(s):
            item = g * per_block + s
            target = jj * per_block + s

            @pl.when((target != k) & jnp.logical_not(at_edge))
            def _():
                down = jnp.where(target < k, 1, 0)
                line_wait(item, down)
                sendbuf[item] = (part[item] + recv[down, item].astype(jnp.float32)).astype(
                    jnp.bfloat16
                )
                line_copy(item, down).start()

            @pl.when(target == k)
            def _():
                @pl.when(k > 0)
                def _():
                    line_wait(item, 0)
                    part[item] = part[item] + recv[0, item].astype(jnp.float32)

                @pl.when(k < n_out - 1)
                def _():
                    line_wait(item, 1)
                    part[item] = part[item] + recv[1, item].astype(jnp.float32)

                @pl.when(to == i)
                def _():
                    landing[i] = part[item].astype(jnp.bfloat16)

                @pl.when(to != i)
                def _():
                    sendbuf[item] = part[item].astype(jnp.bfloat16)
                    fin_copy(to).start()

    def weight_term(dp, dc):
        to = tok_at(dp, dc)
        if dp or dc:
            pltpu.make_async_remote_copy(
                src_ref=acts.at[to],
                dst_ref=acts.at[to],
                send_sem=act_s.at[dp * 2 + dc],
                recv_sem=act_r.at[to],
                device_id={"tok": tok_at(0, 1)},
                device_id_type=MESH,
            ).wait_recv()
        else:
            act_copy.wait()

    def weight_dot(to):
        @pl.loop(0, feats // f_tile)
        def _(t):
            cols = pl.ds(pl.multiple_of(t * f_tile, f_tile), f_tile)
            n_mb = acts.shape[1]
            lhs = acts[to, :, :, cols].reshape(-1, f_tile)
            rhs = jnp.concatenate(
                [cot[to * n_inc + jj, m] for m in range(n_mb) for jj in range(n_inc)], axis=0
            )
            dw[cols, :] += lax.dot_general(
                lhs, rhs, (((0,), (0,)), ((), ())), preferred_element_type=jnp.float32
            )

    def run(fn, low, high):
        @pl.loop(low, high)
        def _(b):
            fn(b)

    first = 2 * n_inc + 2
    run(compute, 0, 2)
    for dp in range(1, pairs):
        g = tok_at(dp, 0) * n_inc + j
        to_core(g).wait_recv()
        for dj in range(1, n_inc):
            to_inc(dp, dj).start()
        to_core(g).start()
    for dj in range(1, n_inc):
        g = i * n_inc + inc_at(dj)
        to_core(g).wait_recv()
        to_core(g).start()
    run(compute, 2, first)
    run(relay, 0, 2)
    for dp in range(1, pairs):
        for dj in range(1, n_inc):
            g = tok_at(dp, 0) * n_inc + inc_at(dj)
            to_core(g).wait_recv()
            to_core(g).start()
    run(compute, first, blocks)
    for dc in range(2):
        weight_term(0, dc)
        weight_dot(tok_at(0, dc))
    run(relay, 2, first)
    for dp in range(1, pairs):
        for dc in range(2):
            weight_term(dp, dc)
    run(lambda d: weight_dot(tok_at(d // 2, d % 2)), 2, n_tok)
    dw_copy = pltpu.make_async_copy(dw, dw_out.at[0], misc_s.at[2])
    dw_copy.start()
    run(relay, first, blocks)

    def out_copy(frm):
        return pltpu.make_async_copy(
            landing.at[frm],
            dx_out.at[:, :, pl.ds(pl.multiple_of(frm * feats, feats), feats)],
            out_s.at[frm],
        )

    out_copy(i).start()
    for d in range(1, n_tok):
        frm = lax.rem(i + d, n_tok)
        pltpu.make_async_remote_copy(
            src_ref=landing.at[frm],
            dst_ref=landing.at[frm],
            send_sem=fin_s.at[frm],
            recv_sem=fin_r.at[frm],
            device_id={"tok": frm},
            device_id_type=MESH,
        ).wait_recv()
        out_copy(frm).start()

    for dp in range(pairs):
        for dj in range(n_inc):
            to_core(tok_at(dp, 0) * n_inc + inc_at(dj)).wait_send()
            if dj:
                to_inc(dp, dj).wait_send()
        if dp:
            to_tok(dp).wait_send()
        for dc in range(2):
            if dp or dc:
                act_send(dp, dc).wait_send()

    @pl.loop(0, n_tok * n_out)
    def _(item):
        @pl.when(item % n_out != k)
        def _():
            down = jnp.where(item % n_out < k, 1, 0)
            line_copy(item, down).wait_send()

    for d in range(1, n_tok):
        fin_copy(lax.rem(i + d, n_tok)).wait_send()
    for d in range(n_tok):
        out_copy(lax.rem(i + d, n_tok)).wait()
    dw_copy.wait()


def solution(mesh):
    sizes = tuple(mesh.shape[name] for name in ("tok", "inc", "outc"))
    n_tok, n_inc, n_out = sizes

    def local(activations, student_out, teacher_out, weight):
        n_mb, rows, depth = student_out.shape
        feats = weight.shape[1]
        chunk = rows * n_inc // n_out
        items = n_tok * n_out
        bf16, f32 = jnp.bfloat16, jnp.float32
        dma = pltpu.SemaphoreType.DMA
        flops = 4 * n_mb * rows * n_inc * n_tok * depth * feats
        return pl.pallas_call(
            functools.partial(kernel, sizes),
            out_shape=(
                jax.ShapeDtypeStruct((n_mb, chunk, n_tok * feats), bf16),
                jax.ShapeDtypeStruct(weight.shape, f32),
            ),
            in_specs=[
                pl.BlockSpec(memory_space=pl.ANY),
                pl.BlockSpec(memory_space=pltpu.VMEM),
                pl.BlockSpec(memory_space=pltpu.VMEM),
                pl.BlockSpec(memory_space=pl.ANY),
            ],
            out_specs=(pl.BlockSpec(memory_space=pl.ANY), pl.BlockSpec(memory_space=pl.ANY)),
            scratch_shapes=[
                pltpu.VMEM((n_tok * n_inc, n_mb, rows, depth), bf16),
                pltpu.VMEM((n_tok, n_mb, activations.shape[1], feats), bf16),
                pltpu.VMEM((items, n_mb, chunk, feats), f32),
                pltpu.VMEM((2, items, n_mb, chunk, feats), bf16),
                pltpu.VMEM((items, n_mb, chunk, feats), bf16),
                pltpu.VMEM((n_tok, n_mb, chunk, feats), bf16),
                pltpu.VMEM((feats, depth), f32),
                pltpu.VMEM(weight.shape, bf16),
                dma((n_tok * n_inc,)),
                dma((n_tok // 2,)),
                dma((n_tok // 2 * n_inc,)),
                dma((n_tok * n_inc,)),
                dma((n_tok,)),
                dma((n_tok,)),
                dma((items,)),
                dma((2, items)),
                dma((n_tok,)),
                dma((n_tok,)),
                dma((n_tok,)),
                dma((3,)),
            ],
            compiler_params=pltpu.CompilerParams(
                collective_id=0, has_side_effects=True, vmem_limit_bytes=62 * 1024 * 1024
            ),
            cost_estimate=pl.CostEstimate(
                flops=flops, bytes_accessed=16 * 1024 * 1024, transcendentals=0
            ),
        )(activations, student_out, teacher_out, weight)

    placed = (
        P(None, "tok", "inc"),
        P(None, ("tok", "inc"), "outc"),
        P(None, ("tok", "inc"), "outc"),
        P("inc", "tok", "outc"),
    )
    return jax.shard_map(
        local,
        mesh=mesh,
        in_specs=placed,
        out_specs=(P(None, ("tok", "outc"), "inc"), P("inc", "tok", "outc")),
        check_vma=False,
    )
```

time: 390 us -> 149 us (0.38)
  waiting for transfers between devices: 337 us -> 0 us
  Pallas kernels: 0 us -> 141 us
  matrix products: 25.7 us -> 0 us
  between operations: 13.8 us -> 0.64 us
  other arithmetic: 4.88 us -> 0 us
    reduce_scatter x2 -> x0, waiting for transfers between devices: 254 us -> none  [the longest x1 128 us: local(): lax.psum_scatter(partial_grad, 'outc', scatter_dimension=1, tiled=True)]
    pallas_call x0 -> x1, Pallas kernels: none -> 141 us  [local(): pl.pallas_call(functools.partial(kernel, sizes), out_shape=(jax.ShapeDtyp...]
    all_gather x2 -> x0, waiting for transfers between devices: 82.4 us -> none  [the longest x1 60.4 us: local(): lax.all_gather(weight, 'tok', axis=1, tiled=True)[0]]
    dot_general x3 -> x0, matrix products: 25.7 us -> none  [the longest x2 14.2 us: batch_term(): jnp.einsum('ti,tc->ic', columns, cotangent[batch_idx], preferred_element_...]
    convert_element_type x2 -> x0, other arithmetic: 4.88 us -> none  [the longest x1 2.69 us: local(): lax.psum_scatter(partial_grad, 'outc', scatter_dimension=1, tiled=True)]
  transfers between devices with their start and end apart: 4 -> 0, of which waited for: 4 -> 0; matrix products, arithmetic and copies ran while one was open for 4% -> 0% of each run, Pallas kernels for 0% -> 0%
where the time goes in v1:
time: 149 us
  Pallas kernels  141 us (95%)
  local copies, waits for them, and re-layouts  7.07 us (5%)
    pallas_call x1, Pallas kernels, local(): pl.pallas_call(functools.partial(kernel, sizes), out_shape=(jax.ShapeDtyp...  141 us
    unnamed x2, local copies, waits for them, and re-layouts  7.07 us

profile of v1, /device:TPU:25, one launch (start us, length us, event | category | flops | bytes accessed | tf_op | source)
XLA Modules:
  0.0 149.0 jit_solution(3809553769012089454)
XLA Ops:
  0.6 141.3 %shard_map.59 = (bf16[2,64,4096]{2,1,0:T(8,128)(2,1)}, f32[1,1024,1024]{2,1,0:T(8,128)}) custom-call(bf16[2,256,4096]{2,1,0:T(8,128)(2,1)} %act.1, bf16[2,128,1024]{2,1,0:T(8,128)(2,1)} %student.1, bf16[2,128,1024]{2,1,0:T(8,128)(2,1)} %teacher.1, bf16[1,1024,1024]{2,1,0:T(8,128)(2,1)} %weight.1), custom_call_target="tpu_custom_call" | custom-call | flops 8589934592 | bytes 16777216 | tf_op jit(solution)/shard_map/pallas_call | solution.py:368
  141.9 2.3 %copy.8 = bf16[2,64,4096]{2,1,0:T(8,128)(2,1)} copy(bf16[2,64,4096]{2,1,0:T(8,128)(2,1)} %get-tuple-element.4) | data formatting | bytes 2097152
  144.2 4.8 %copy.9 = f32[1,1024,1024]{2,1,0:T(8,128)} copy(f32[1,1024,1024]{2,1,0:T(8,128)} %get-tuple-element.5) | data formatting | bytes 8388608

commit v2 on v1

--- a/solution.py
+++ b/solution.py
@@ -184,18 +184,6 @@
             for s in range(per_block):
                 part[g * per_block + s, :, :, cols] = res[:, s]
 
-        @pl.when(at_edge)
-        def _():
-            @pl.loop(0, per_block)
-            def _(s):
-                item = g * per_block + s
-                target = jj * per_block + s
-
-                @pl.when(target != k)
-                def _():
-                    sendbuf[item] = part[item].astype(jnp.bfloat16)
-                    line_copy(item, jnp.where(target < k, 1, 0)).start()
-
     def fin_copy(to):
         return pltpu.make_async_remote_copy(
             src_ref=sendbuf.at[to * n_out + k],
@@ -206,25 +194,55 @@
             device_id_type=MESH,
         )
 
-    def relay(b):
-        to, jj, g, dc = block_of(b)
-
-        @pl.loop(0, per_block)
-        def _(s):
-            item = g * per_block + s
-            target = jj * per_block + s
-
-            @pl.when((target != k) & jnp.logical_not(at_edge))
+    low = 2 * j < n_inc
+
+    def group_first(q):
+        r = jnp.maximum(q - 1, 0)
+        tail = q > pairs * (n_inc - 1)
+        dp = jnp.where(tail, q - pairs * (n_inc - 1), r // max(n_inc - 1, 1))
+        dj = jnp.where(tail | (q == 0), 0, 1 + r % max(n_inc - 1, 1))
+        return jnp.where(q == 0, 0, dp), dj
+
+    def group_second(q):
+        return q % pairs, q // pairs
+
+    def group(q, down):
+        first, second = group_first(q), group_second(q)
+        use = jnp.logical_not(low) if down else low
+        return jnp.where(use, first[0], second[0]), jnp.where(use, first[1], second[1])
+
+    def item_at(q, n, down):
+        dp, dj = group(q, down)
+        s, dc = n // 2, n % 2
+        if not down:
+            s = per_block - 1 - s
+        jj = inc_at(dj)
+        return (tok_at(dp, dc) * n_inc + jj) * per_block + s, jj * per_block + s
+
+    def emit(q):
+        for down in range(2):
+
+            @pl.when(k == (n_out - 1 if down else 0))
             def _():
-                down = jnp.where(target < k, 1, 0)
-                line_wait(item, down)
-                sendbuf[item] = (part[item] + recv[down, item].astype(jnp.float32)).astype(
-                    jnp.bfloat16
-                )
-                line_copy(item, down).start()
-
-            @pl.when(target == k)
-            def _():
+                @pl.loop(0, 2 * per_block)
+                def _(n):
+                    item, target = item_at(q, n, down)
+
+                    @pl.when(target != k)
+                    def _():
+                        sendbuf[item] = part[item].astype(jnp.bfloat16)
+                        line_copy(item, down).start()
+
+    def finish(dp, dj):
+        jj = inc_at(dj)
+
+        @pl.when(jj == k // per_block)
+        def _():
+            @pl.loop(0, 2)
+            def _(dc):
+                to = tok_at(dp, dc)
+                item = to * n_out + k
+
                 @pl.when(k > 0)
                 def _():
                     line_wait(item, 0)
@@ -243,6 +261,34 @@
                 def _():
                     sendbuf[item] = part[item].astype(jnp.bfloat16)
                     fin_copy(to).start()
+
+    def relay(q):
+        @pl.when(jnp.logical_not(at_edge))
+        def _():
+            @pl.loop(0, 2 * per_block)
+            def _(n):
+                for down in range(2):
+                    item, target = item_at(q, n, down)
+
+                    @pl.when(target < k if down else target > k)
+                    def _():
+                        line_wait(item, down)
+                        sendbuf[item] = (
+                            part[item] + recv[down, item].astype(jnp.float32)
+                        ).astype(jnp.bfloat16)
+                        line_copy(item, down).start()
+
+        dp, dj = group_first(q)
+
+        @pl.when(dj == 0)
+        def _():
+            finish(dp, dj)
+
+        dp, dj = group_second(q)
+
+        @pl.when(dj > 0)
+        def _():
+            finish(dp, dj)
 
     def weight_term(dp, dc):
         to = tok_at(dp, dc)
@@ -276,8 +322,9 @@
         def _(b):
             fn(b)
 
-    first = 2 * n_inc + 2
+    first, groups = min(2 * n_inc + 2, blocks), pairs * n_inc
     run(compute, 0, 2)
+    emit(0)
     for dp in range(1, pairs):
         g = tok_at(dp, 0) * n_inc + j
         to_core(g).wait_recv()
@@ -289,24 +336,26 @@
         to_core(g).wait_recv()
         to_core(g).start()
     run(compute, 2, first)
-    run(relay, 0, 2)
+    emit(1)
     for dp in range(1, pairs):
         for dj in range(1, n_inc):
             g = tok_at(dp, 0) * n_inc + inc_at(dj)
             to_core(g).wait_recv()
             to_core(g).start()
     run(compute, first, blocks)
+    run(emit, 2, groups)
+    run(relay, 0, 1)
     for dc in range(2):
         weight_term(0, dc)
         weight_dot(tok_at(0, dc))
-    run(relay, 2, first)
+    run(relay, 1, groups - 1)
     for dp in range(1, pairs):
         for dc in range(2):
             weight_term(dp, dc)
     run(lambda d: weight_dot(tok_at(d // 2, d % 2)), 2, n_tok)
     dw_copy = pltpu.make_async_copy(dw, dw_out.at[0], misc_s.at[2])
     dw_copy.start()
-    run(relay, first, blocks)
+    run(relay, groups - 1, groups)
 
     def out_copy(frm):
         return pltpu.make_async_copy(

time: 149 us -> 137 us (0.919); the launches traced: 149 us -> 135 us
  Pallas kernels: 141 us -> 127 us
    pallas_call x1, Pallas kernels: 141 us -> 127 us  [local(): pl.pallas_call(functools.partial(kernel, sizes), out_shape=(jax.ShapeDtyp...]
where the time goes in v2:
time: 137 us; the launch traced here: 135 us
  Pallas kernels  127 us (93%)
  local copies, waits for them, and re-layouts  7.07 us (5%)
    pallas_call x1, Pallas kernels, local(): pl.pallas_call(functools.partial(kernel, sizes), out_shape=(jax.ShapeDtyp...  127 us
    unnamed x2, local copies, waits for them, and re-layouts  7.07 us

profile of v2, /device:TPU:25, one launch (start us, length us, event | category | flops | bytes accessed | tf_op | source)
XLA Modules:
  0.0 134.5 jit_solution(10261511180480914231)
XLA Ops:
  0.6 126.8 %shard_map.59 = (bf16[2,64,4096]{2,1,0:T(8,128)(2,1)}, f32[1,1024,1024]{2,1,0:T(8,128)}) custom-call(bf16[2,256,4096]{2,1,0:T(8,128)(2,1)} %act.1, bf16[2,128,1024]{2,1,0:T(8,128)(2,1)} %student.1, bf16[2,128,1024]{2,1,0:T(8,128)(2,1)} %teacher.1, bf16[1,1024,1024]{2,1,0:T(8,128)(2,1)} %weight.1), custom_call_target="tpu_custom_call" | custom-call | flops 8589934592 | bytes 16777216 | tf_op jit(solution)/shard_map/pallas_call | solution.py:417
  127.4 2.3 %copy.8 = bf16[2,64,4096]{2,1,0:T(8,128)(2,1)} copy(bf16[2,64,4096]{2,1,0:T(8,128)(2,1)} %get-tuple-element.4) | data formatting | bytes 2097152
  129.7 4.8 %copy.9 = f32[1,1024,1024]{2,1,0:T(8,128)} copy(f32[1,1024,1024]{2,1,0:T(8,128)} %get-tuple-element.5) | data formatting | bytes 8388608

commit v3 on v2

--- a/solution.py
+++ b/solution.py
@@ -278,6 +278,7 @@
                         ).astype(jnp.bfloat16)
                         line_copy(item, down).start()
 
+    def finish_group(q):
         dp, dj = group_first(q)
 
         @pl.when(dj == 0)
@@ -337,6 +338,7 @@
         to_core(g).start()
     run(compute, 2, first)
     emit(1)
+    relay(0)
     for dp in range(1, pairs):
         for dj in range(1, n_inc):
             g = tok_at(dp, 0) * n_inc + inc_at(dj)
@@ -344,18 +346,20 @@
             to_core(g).start()
     run(compute, first, blocks)
     run(emit, 2, groups)
-    run(relay, 0, 1)
+    run(relay, 1, 2)
+    finish_group(0)
+    run(relay, 2, groups)
     for dc in range(2):
         weight_term(0, dc)
         weight_dot(tok_at(0, dc))
-    run(relay, 1, groups - 1)
+    run(finish_group, 1, groups - 1)
     for dp in range(1, pairs):
         for dc in range(2):
             weight_term(dp, dc)
     run(lambda d: weight_dot(tok_at(d // 2, d % 2)), 2, n_tok)
     dw_copy = pltpu.make_async_copy(dw, dw_out.at[0], misc_s.at[2])
     dw_copy.start()
-    run(relay, groups - 1, groups)
+    run(finish_group, groups - 1, groups)
 
     def out_copy(frm):
         return pltpu.make_async_copy(

time: 137 us -> 128 us (0.934)
  the two profiles are of different devices: /device:TPU:25 before, /device:TPU:13 now
where the time goes in v3:
time: 128 us
  Pallas kernels  120 us (94%)
  local copies, waits for them, and re-layouts  7.07 us (6%)
    pallas_call x1, Pallas kernels, local(): pl.pallas_call(functools.partial(kernel, sizes), out_shape=(jax.ShapeDtyp...  120 us
    unnamed x2, local copies, waits for them, and re-layouts  7.07 us

profile of v3, /device:TPU:13, one launch (start us, length us, event | category | flops | bytes accessed | tf_op | source)
XLA Modules:
  0.0 127.8 jit_solution(14922359182988475284)
XLA Ops:
  0.6 120.1 %shard_map.59 = (bf16[2,64,4096]{2,1,0:T(8,128)(2,1)}, f32[1,1024,1024]{2,1,0:T(8,128)}) custom-call(bf16[2,256,4096]{2,1,0:T(8,128)(2,1)} %act.1, bf16[2,128,1024]{2,1,0:T(8,128)(2,1)} %student.1, bf16[2,128,1024]{2,1,0:T(8,128)(2,1)} %teacher.1, bf16[1,1024,1024]{2,1,0:T(8,128)(2,1)} %weight.1), custom_call_target="tpu_custom_call" | custom-call | flops 8589934592 | bytes 16777216 | tf_op jit(solution)/shard_map/pallas_call | solution.py:421
  120.7 2.3 %copy.8 = bf16[2,64,4096]{2,1,0:T(8,128)(2,1)} copy(bf16[2,64,4096]{2,1,0:T(8,128)(2,1)} %get-tuple-element.4) | data formatting | bytes 2097152
  123.0 4.8 %copy.9 = f32[1,1024,1024]{2,1,0:T(8,128)} copy(f32[1,1024,1024]{2,1,0:T(8,128)} %get-tuple-element.5) | data formatting | bytes 8388608
